TPU v7x, 32 devices: a whole 2x2x4 slice. The times are simulated.
32 devices in a mesh: videos: 2 (over y), rows: 4 (over z), cols: 4 (over x, core).
Axes of the slice: x: 2, y: 2, z: 4, core: 2. Of those that a mesh axis runs over, the one named last changes fastest.
Arguments:
- hidden: bfloat16 [2, 16, 128, 384], P('videos', 'rows', 'cols'), parts along dimension 0, may hold values from -40 to 40
- frame_cache: bfloat16 [2, 2, 16, 128, 384], P('videos', None, 'rows', 'cols'), parts along dimension 0, may hold values from -6 to 6
- shortcut: bfloat16 [2, 16, 128, 384], P('videos', 'rows', 'cols'), parts along dimension 0, may hold values from -40 to 40
- gain_one: float32 [384], replicated, may hold values from 0.5 to 1.5
- conv_weight: bfloat16 [3, 3, 3, 384, 384], replicated, may hold values from -0.0625 to 0.0625
- conv_bias: float32 [384], replicated, may hold values from -2 to 2
- gain_two: float32 [384], replicated, may hold values from 0.5 to 1.5
- query_weight: bfloat16 [384, 384], replicated, may hold values from -1 to 1
- query_bias: float32 [384], replicated, may hold values from -3 to 3
- key_weight: bfloat16 [384, 384], replicated, may hold values from -1 to 1
- value_weight: bfloat16 [384, 384], replicated, may hold values from -0.3125 to 0.3125
- value_bias: float32 [384], replicated, may hold values from -3 to 3
- out_weight: bfloat16 [384, 384], replicated, may hold values from -0.3125 to 0.3125
- out_bias: float32 [384], replicated, may hold values from -2 to 2
Outputs:
- decoded: bfloat16 [2, 16, 128, 384], P('videos', 'rows', 'cols'), parts along dimension 0
There are 2 independent parts, one for each index of `videos`. A program takes and returns all parts, laid end to end along the dimension named above; an argument that names none is the same for every part. Nothing has to cross between parts.
All inputs are finite; a program needn't handle non-finite values.
Results may differ from a plain program's by a relative error of at most 0.0065.
Values may be sent and summed in bfloat16 or wider, within the bound.
No kernel may reach another device: no remote copies, remote signals or barrier semaphores. Data moves between devices by JAX's collectives and lax.ppermute only.
A program may use at most 128 MiB of HBM per device.

v0:
```python
import jax
import jax.numpy as jnp
from jax import lax
from jax.sharding import PartitionSpec as P

norm_epsilon = 1e-06


def padded(cells, sides, width):
    for axis, dim in sides:
        count = lax.axis_size(axis)
        ends = count - 1
        head = lax.slice_in_dim(cells, 0, width, axis=dim)
        tail = lax.slice_in_dim(cells, cells.shape[dim] - width, cells.shape[dim], axis=dim)
        cells = jnp.concatenate(
            [
                lax.ppermute(tail, axis, [(i, (i + 1) % count) for i in range(ends)]),
                cells,
                lax.ppermute(head, axis, [((i + 1) % count, i) for i in range(ends)]),
            ],
            axis=dim,
        )
    return cells


def normalize(field_rows, gain):
    mean_square = jnp.mean(field_rows * field_rows, axis=1, keepdims=True)
    return field_rows * lax.rsqrt(mean_square + norm_epsilon) * gain


def per_device(
    hidden,
    frame_cache,
    shortcut,
    gain_one,
    conv_weight,
    conv_bias,
    gain_two,
    query_weight,
    query_bias,
    key_weight,
    value_weight,
    value_bias,
    out_weight,
    out_bias,
):
    tile_rows = hidden.shape[1]
    tile_cols = hidden.shape[2]
    channels = hidden.shape[3]
    current = hidden[0].reshape(tile_rows * tile_cols, channels).astype(jnp.float32)
    activated = jax.nn.silu(normalize(current, gain_one)).astype(jnp.bfloat16)
    stacked = jnp.concatenate(
        [frame_cache[0], activated.reshape(1, tile_rows, tile_cols, channels)], axis=0
    )
    rimmed = padded(stacked, (("rows", 1), ("cols", 2)), 1)
    convolved = (
        lax.conv_general_dilated(
            rimmed[None],
            conv_weight,
            (1, 1, 1),
            "VALID",
            dimension_numbers=("NDHWC", "DHWIO", "NDHWC"),
            preferred_element_type=jnp.float32,
        )[0, 0]
        + conv_bias
    )
    mixed = (
        (shortcut[0].astype(jnp.float32) + convolved)
        .astype(jnp.bfloat16)
        .reshape(tile_rows * tile_cols, channels)
    )
    normed = normalize(mixed.astype(jnp.float32), gain_two).astype(jnp.bfloat16)
    queries = (
        jnp.dot(normed, query_weight, preferred_element_type=jnp.float32) + query_bias
    ).astype(jnp.bfloat16)
    score_scale = float(channels) ** (-0.5)
    query_count = queries.shape[0]
    piece = lax.all_gather(normed, ("rows", "cols"), axis=0, tiled=True)
    key_rows = jnp.dot(piece, key_weight, preferred_element_type=jnp.float32).astype(jnp.bfloat16)
    value_rows = (
        jnp.dot(piece, value_weight, preferred_element_type=jnp.float32) + value_bias
    ).astype(jnp.bfloat16)
    running_max = jnp.full((query_count,), -1e30, jnp.float32)
    scores = (
        jnp.einsum("qc,kc->qk", queries, key_rows, preferred_element_type=jnp.float32) * score_scale
    )
    new_max = jnp.maximum(running_max, jnp.max(scores, axis=1))
    expos = jnp.exp(scores - new_max[:, None])
    new_sum = jnp.sum(expos, axis=1)
    new_weighted = jnp.dot(
        expos.astype(jnp.bfloat16), value_rows, preferred_element_type=jnp.float32
    )
    attended = (new_weighted / new_sum[:, None]).astype(jnp.bfloat16)
    projected = jnp.dot(attended, out_weight, preferred_element_type=jnp.float32) + out_bias
    decoded = (mixed.astype(jnp.float32) + projected).astype(jnp.bfloat16)
    return decoded.reshape(1, tile_rows, tile_cols, channels)


def solution(mesh):
    placed = (
        P("videos", "rows", "cols", None),
        P("videos", None, "rows", "cols", None),
        P("videos", "rows", "cols", None),
        P(),
        P(),
        P(),
        P(),
        P(),
        P(),
        P(),
        P(),
        P(),
        P(),
        P(),
    )
    return jax.shard_map(
        per_device,
        mesh=mesh,
        in_specs=placed,
        out_specs=P("videos", "rows", "cols", None),
        check_vma=False,
    )
```

profile of v0, /device:TPU:0, one launch (start us, length us, event | category | flops | bytes accessed | tf_op | source)
XLA Modules:
  0.0 91.4 jit_solution(13943314025765096930)
XLA Ops:
  6.5 1.0 %fusion.18 = f32[4,32]{1,0:T(4,128)S(1)} fusion(bf16[1,4,32,384]{3,2,1,0:T(8,128)(2,1)} %param.14), kind=kLoop, calls=%fused_computation.28 | loop fusion | flops 147328 | bytes 98816 | tf_op jit(solution)/shard_map/reduce_sum | solution.py:27
  7.6 1.0 %fusion.25 = bf16[1,4,32,384]{3,2,1,0:T(8,128)(2,1)S(1)} fusion(bf16[1,4,32,384]{3,2,1,0:T(8,128)(2,1)} %param.14, f32[384]{0:T(512)} %param.17, f32[4,32]{1,0:T(4,128)S(1)} %add_rsqrt_fusion.1), kind=kLoop, calls=%fused_computation.35 | loop fusion | flops 393216 | bytes 198656 | tf_op jit(solution)/shard_map/convert_element_type | solution.py:51
  8.6 0.9 pad_maximum_fusion.1
  9.5 5.0 %collective-permute-start = (bf16[3,1,32,384]{3,2,1,0:T(8,128)(2,1)S(1)}, bf16[3,1,32,384]{3,2,1,0:T(8,128)(2,1)S(1)}, u32[]{:S(2)}, u32[]{:S(2)}) collective-permute-start(bf16[3,1,32,384]{3,2,1,0:T(8,128)(2,1)S(1)} %get-tuple-element.9), channel_id=1, source_target_pairs={{0,4},{4,8},{8,12},{1,5},{5,9},{9,13},{2,6},{6,10},{10,14},{3,7},{... | collective-permute-start | bytes 221192 | tf_op jit(solution)/shard_map/ppermute | solution.py:17
  14.4 1.3 %collective-permute-start.1 = (bf16[3,1,32,384]{3,2,1,0:T(8,128)(2,1)S(1)}, bf16[3,1,32,384]{3,2,1,0:T(8,128)(2,1)S(1)}, u32[]{:S(2)}, u32[]{:S(2)}) collective-permute-start(bf16[3,1,32,384]{3,2,1,0:T(8,128)(2,1)S(1)} %get-tuple-element.10), channel_id=1, source_target_pairs={{4,0},{8,4},{12,8},{5,1},{9,5},{13,9},{6,2},{10,6},{14,10},{7,3},{... | collective-permute-start | bytes 221192 | tf_op jit(solution)/shard_map/ppermute | solution.py:19
  15.7 0.7 collective-permute-done
  16.4 4.3 %collective-permute-done.1 = bf16[3,1,32,384]{3,2,1,0:T(8,128)(2,1)S(1)} collective-permute-done((bf16[3,1,32,384]{3,2,1,0:T(8,128)(2,1)S(1)}, bf16[3,1,32,384]{3,2,1,0:T(8,128)(2,1)S(1)}, u32[]{:S(2)}, u32[]{:S(2)}) %collective-permute-start.1) | collective-permute-done | bytes 73760 | tf_op jit(solution)/shard_map/ppermute | solution.py:19
  20.7 0.9 pad_maximum_fusion.5
  21.6 1.3 %collective-permute-start.2 = (bf16[3,6,1,384]{3,2,1,0:T(2,128)(2,1)S(1)}, bf16[3,6,1,384]{3,2,1,0:T(2,128)(2,1)S(1)}, u32[]{:S(2)}, u32[]{:S(2)}) collective-permute-start(bf16[3,6,1,384]{3,2,1,0:T(2,128)(2,1)S(1)} %get-tuple-element.7), channel_id=1, source_target_pairs={{0,1},{1,2},{2,3},{4,5},{5,6},{6,7},{8,9},{9,10},{10,11},{12,13},{... | collective-permute-start | bytes 41480 | tf_op jit(solution)/shard_map/ppermute | solution.py:17
  22.9 1.3 %collective-permute-start.3 = (bf16[3,6,1,384]{3,2,1,0:T(2,128)(2,1)S(1)}, bf16[3,6,1,384]{3,2,1,0:T(2,128)(2,1)S(1)}, u32[]{:S(2)}, u32[]{:S(2)}) collective-permute-start(bf16[3,6,1,384]{3,2,1,0:T(2,128)(2,1)S(1)} %get-tuple-element.8), channel_id=1, source_target_pairs={{1,0},{2,1},{3,2},{5,4},{6,5},{7,6},{9,8},{10,9},{11,10},{13,12},{... | collective-permute-start | bytes 41480 | tf_op jit(solution)/shard_map/ppermute | solution.py:19
  24.2 3.5 %collective-permute-done.3 = bf16[3,6,1,384]{3,2,1,0:T(2,128)(2,1)S(1)} collective-permute-done((bf16[3,6,1,384]{3,2,1,0:T(2,128)(2,1)S(1)}, bf16[3,6,1,384]{3,2,1,0:T(2,128)(2,1)S(1)}, u32[]{:S(2)}, u32[]{:S(2)}) %collective-permute-start.3) | collective-permute-done | bytes 13856 | tf_op jit(solution)/shard_map/ppermute | solution.py:19
  27.7 1.2 %maximum_bitcast_fusion = bf16[3,6,1,34,384]{4,3,1,0,2:T(8,128)(2,1)S(1)} fusion(bf16[3,6,1,384]{3,2,1,0:T(2,128)(2,1)S(1)} %collective-permute-done.3, bf16[3,1,32,384]{3,2,1,0:T(8,128)(2,1)S(1)} %collective-permute-done.1, bf16[1,4,32,384]{3,2,1,0:T(8,128)(2,1)S(1)} %fusion.25, bf16[2,4,32,384]{3,2,1,0:T(8,128)(2,1)} %bitcast.40, ...), kind=kLoop, calls=%fused_computation.22 | loop fusion | flops 2820096 | bytes 940032 | tf_op jit(solution)/shard_map/broadcast_in_dim | solution.py:58
  29.0 0.1 pad.clone
  29.3 0.4 copy-done.10
  29.7 5.2 %convolution_select_fusion = f32[1,4,8,5,384]{4,2,3,1,0:T(8,128)S(1)} fusion(bf16[3,3,3,384,384]{4,3,2,1,0:T(8,128)(2,1)} %param.18, bf16[3,6,1,7,2,384]{5,3,4,1,0,2:T(8,128)(2,1)S(1)} %slice.18, bf16[3,6,1,8,5,384]{5,3,4,1,0,2:T(8,128)(2,1)S(1)} %copy.41, pred[8,5]{0,1:T(8,128)(4,1)S(1)} %copy-done.10), kind=kOutput, calls=%fused_computation.9 | convolution fusion | flops 1276403712 | bytes 8954920 | tf_op jit(solution)/shard_map/conv_general_dilated | solution.py:57
  35.1 0.1 multiply_reduce_fusion
  35.3 0.3 copy-done.5
  35.6 0.7 fusion.27
  36.3 1.1 %fusion.3 = bf16[128,384]{1,0:T(8,128)(2,1)S(1)} fusion(bf16[128,384]{1,0:T(8,128)(2,1)} %get-tuple-element.5, bf16[384,384]{1,0:T(8,128)(2,1)S(1)} %copy-done.3, f32[384]{0:T(512)S(1)} %copy-done.6), kind=kOutput, calls=%fused_computation.10 | convolution fusion | flops 37847040 | bytes 493056 | tf_op jit(solution)/shard_map/dot_general | solution.py:74
  37.5 40.1 %all-gather.2.cloned.1.call-done = bf16[2048,384]{1,0:T(8,128)(2,1)} async-done(((bf16[128,384]{1,0:T(8,128)(2,1)}), bf16[2048,384]{1,0:T(8,128)(2,1)}) %all-gather.2.cloned.1.call-update) | async-done | bytes 1572880 | tf_op jit(solution)/shard_map/all_gather | solution.py:78
  77.6 3.1 %fusion.36 = (f32[128]{0:T(128)S(1)}, f32[128,2048]{1,0:T(8,128)S(1)}) fusion(bf16[128,384]{1,0:T(8,128)(2,1)S(1)} %fusion.3, bf16[2048,384]{1,0:T(8,128)(2,1)} %all-gather.2.cloned.1.call-done, bf16[384,384]{1,0:T(8,128)(2,1)S(1)} %copy-done), kind=kOutput, calls=%fused_computation.57 | convolution fusion | flops 806616960 | bytes 3015168 | tf_op jit(solution)/shard_map/qc,kc->qk/dot_general | solution.py:85
  80.7 0.3 fusion.7
  81.1 2.6 %fusion.6 = bf16[128,384]{1,0:T(8,128)(2,1)S(1)} fusion(bf16[2048,384]{1,0:T(8,128)(2,1)S(1)} %copy-done.8, bf16[384,384]{1,0:T(8,128)(2,1)} %param.24, f32[384]{0:T(512)S(1)} %copy-done.9, f32[128,2048]{1,0:T(8,128)S(1)} %get-tuple-element.12, f32[128]{0:T(128)S(1)} %broadcast_maximum_fusion, f32[128]{0:T(128)S(1)} %fusion.7), kind=kOutput, calls=%fused_computation.13 | convolution fusion | flops 807501824 | bytes 3017216 | tf_op jit(solution)/shard_map/dot_general | solution.py:90
  83.7 0.9 fusion.4
  (33 shorter events, 0.5 us)
Async XLA Ops:
  6.5 71.1 %copy-start = (bf16[384,384]{1,0:T(8,128)(2,1)S(1)}, bf16[384,384]{1,0:T(8,128)(2,1)}, u32[]{:S(2)}) copy-start(bf16[384,384]{1,0:T(8,128)(2,1)} %param.23) | copy-start | bytes 884740
  6.5 71.1 %all-gather.2.cloned.1.call-start = ((), (), s32[]{:S(2)}) async-start(), calls=%async_computation | async-start | bytes 1671168 | tf_op jit(solution)/shard_map/all_gather | solution.py:78
  9.5 6.9 %collective-permute-start = (bf16[3,1,32,384]{3,2,1,0:T(8,128)(2,1)S(1)}, bf16[3,1,32,384]{3,2,1,0:T(8,128)(2,1)S(1)}, u32[]{:S(2)}, u32[]{:S(2)}) collective-permute-start(bf16[3,1,32,384]{3,2,1,0:T(8,128)(2,1)S(1)} %get-tuple-element.9), channel_id=1, source_target_pairs={{0,4},{4,8},{8,12},{1,5},{5,9},{9,13},{2,6},{6,10},{10,14},{3,7},{... | collective-permute-start | bytes 221192 | tf_op jit(solution)/shard_map/ppermute | solution.py:17
  14.4 6.2 %collective-permute-start.1 = (bf16[3,1,32,384]{3,2,1,0:T(8,128)(2,1)S(1)}, bf16[3,1,32,384]{3,2,1,0:T(8,128)(2,1)S(1)}, u32[]{:S(2)}, u32[]{:S(2)}) collective-permute-start(bf16[3,1,32,384]{3,2,1,0:T(8,128)(2,1)S(1)} %get-tuple-element.10), channel_id=1, source_target_pairs={{4,0},{8,4},{12,8},{5,1},{9,5},{13,9},{6,2},{10,6},{14,10},{7,3},{... | collective-permute-start | bytes 221192 | tf_op jit(solution)/shard_map/ppermute | solution.py:19
  21.6 2.6 %collective-permute-start.2 = (bf16[3,6,1,384]{3,2,1,0:T(2,128)(2,1)S(1)}, bf16[3,6,1,384]{3,2,1,0:T(2,128)(2,1)S(1)}, u32[]{:S(2)}, u32[]{:S(2)}) collective-permute-start(bf16[3,6,1,384]{3,2,1,0:T(2,128)(2,1)S(1)} %get-tuple-element.7), channel_id=1, source_target_pairs={{0,1},{1,2},{2,3},{4,5},{5,6},{6,7},{8,9},{9,10},{10,11},{12,13},{... | collective-permute-start | bytes 41480 | tf_op jit(solution)/shard_map/ppermute | solution.py:17
  22.9 4.8 %collective-permute-start.3 = (bf16[3,6,1,384]{3,2,1,0:T(2,128)(2,1)S(1)}, bf16[3,6,1,384]{3,2,1,0:T(2,128)(2,1)S(1)}, u32[]{:S(2)}, u32[]{:S(2)}) collective-permute-start(bf16[3,6,1,384]{3,2,1,0:T(2,128)(2,1)S(1)} %get-tuple-element.8), channel_id=1, source_target_pairs={{1,0},{2,1},{3,2},{5,4},{6,5},{7,6},{9,8},{10,9},{11,10},{13,12},{... | collective-permute-start | bytes 41480 | tf_op jit(solution)/shard_map/ppermute | solution.py:19
  29.0 0.7 copy-start.10
  29.7 5.4 %copy-start.1 = (bf16[1,4,32,384]{3,2,1,0:T(8,128)(2,1)S(1)}, bf16[1,4,32,384]{3,2,1,0:T(8,128)(2,1)}, u32[]{:S(2)}) copy-start(bf16[1,4,32,384]{3,2,1,0:T(8,128)(2,1)} %param.16) | copy-start | bytes 294916
  29.7 5.4 %copy-start.4 = (f32[384]{0:T(512)S(1)}, f32[384]{0:T(512)}, u32[]{:S(2)}) copy-start(f32[384]{0:T(512)} %param.19) | copy-start | bytes 4612
  34.9 0.7 copy-start.5
  34.9 1.4 %copy-start.3 = (bf16[384,384]{1,0:T(8,128)(2,1)S(1)}, bf16[384,384]{1,0:T(8,128)(2,1)}, u32[]{:S(2)}) copy-start(bf16[384,384]{1,0:T(8,128)(2,1)} %param.21) | copy-start | bytes 884740
  34.9 1.4 %copy-start.6 = (f32[384]{0:T(512)S(1)}, f32[384]{0:T(512)}, u32[]{:S(2)}) copy-start(f32[384]{0:T(512)} %param.22) | copy-start | bytes 4612
  37.4 43.6 %copy-start.9 = (f32[384]{0:T(512)S(1)}, f32[384]{0:T(512)}, u32[]{:S(2)}) copy-start(f32[384]{0:T(512)} %param.25) | copy-start | bytes 4612
  77.6 3.5 %copy-start.8 = (bf16[2048,384]{1,0:T(8,128)(2,1)S(1)}, bf16[2048,384]{1,0:T(8,128)(2,1)}, u32[]{:S(2)}) copy-start(bf16[2048,384]{1,0:T(8,128)(2,1)} %all-gather.2.cloned.1.call-done) | copy-start | bytes 4718596
  81.1 2.6 %copy-start.2 = (bf16[384,384]{1,0:T(8,128)(2,1)S(1)}, bf16[384,384]{1,0:T(8,128)(2,1)}, u32[]{:S(2)}) copy-start(bf16[384,384]{1,0:T(8,128)(2,1)} %param.26) | copy-start | bytes 884740
  81.1 2.6 %copy-start.7 = (f32[384]{0:T(512)S(1)}, f32[384]{0:T(512)}, u32[]{:S(2)}) copy-start(f32[384]{0:T(512)} %param.27) | copy-start | bytes 4612
Sparse Core Ops, SparseCore 0:
  36.4 41.1 all-gather.1
where the time goes:
time: 91.8 us; the launch traced here: 91.4 us
  waiting for transfers between devices  48.6 us (53%)
  between operations  13.7 us (15%)
  matrix products  12.9 us (14%)
  starting transfers between devices  8.84 us (10%)
  other arithmetic  6.13 us (7%)
  local copies, waits for them, and re-layouts  1.27 us (1%)
    all_gather x1, waiting for transfers between devices, per_device(): piece = lax.all_gather(normed, ('rows', 'cols'), axis=0, tiled=True)  40.1 us
    ppermute x2, waiting for transfers between devices, padded(): lax.ppermute(head, axis, [((i + 1) % count, i) for i in range(ends)])  7.79 us
    ppermute x2, starting transfers between devices, padded(): lax.ppermute(tail, axis, [(i, (i + 1) % count) for i in range(ends)])  6.25 us
    conv_general_dilated x1, matrix products, per_device(): lax.conv_general_dilated(rimmed[None], conv_weight, (1, 1, 1), 'VALID', d...  5.21 us
    dot_general x1, matrix products, per_device(): jnp.einsum('qc,kc->qk', queries, key_rows, preferred_element_type=jnp.flo...  3.13 us
    ppermute x2, starting transfers between devices, padded(): lax.ppermute(head, axis, [((i + 1) % count, i) for i in range(ends)])  2.58 us
    dot_general x1, matrix products, per_device(): jnp.dot(expos.astype(jnp.bfloat16), value_rows, preferred_element_type=jn...  2.56 us
  transfers between devices with their start and end apart: 5, of which 4 were waited for; matrix products, arithmetic and copies ran while one was open for 1% of the time, Pallas kernels for 0%

commit v1 on v0

--- a/solution.py
+++ b/solution.py
@@ -75,7 +75,28 @@
     ).astype(jnp.bfloat16)
     score_scale = float(channels) ** (-0.5)
     query_count = queries.shape[0]
-    piece = lax.all_gather(normed, ("rows", "cols"), axis=0, tiled=True)
+    ways, here, step = (
+        lax.axis_size(("rows", "cols")),
+        lax.axis_index(("rows", "cols")),
+        normed.shape[0],
+    )
+    lengths = [n * ways if d == 0 else n for d, n in enumerate(normed.shape)]
+    piece = lax.dynamic_update_slice_in_dim(
+        jnp.zeros(lengths, normed.dtype), normed, here * step, axis=0
+    )
+    going_up = going_down = normed
+    for far in range(1, ways // 2 + 1):
+        going_up = lax.ppermute(
+            going_up, ("rows", "cols"), [(d, (d + 1) % ways) for d in range(ways)]
+        )
+        piece = lax.dynamic_update_slice_in_dim(piece, going_up, (here - far) % ways * step, axis=0)
+        if 2 * far < ways:
+            going_down = lax.ppermute(
+                going_down, ("rows", "cols"), [(d, (d - 1) % ways) for d in range(ways)]
+            )
+            piece = lax.dynamic_update_slice_in_dim(
+                piece, going_down, (here + far) % ways * step, axis=0
+            )
     key_rows = jnp.dot(piece, key_weight, preferred_element_type=jnp.float32).astype(jnp.bfloat16)
     value_rows = (
         jnp.dot(piece, value_weight, preferred_element_type=jnp.float32) + value_bias

time: 91.8 us -> 86.2 us (0.939)
  starting transfers between devices: 8.84 us -> 44.3 us
  waiting for transfers between devices: 48.6 us -> 24.3 us
  between operations: 13.7 us -> 0.64 us
  matrix products: 12.9 us -> 10.4 us
  other arithmetic: 6.13 us -> 4.6 us
    all_gather x1 -> x0, waiting for transfers between devices: 40.1 us -> none  [per_device(): piece = lax.all_gather(normed, ('rows', 'cols'), axis=0, tiled=True)]
    ppermute x0 -> x15, starting transfers between devices: none -> 33.1 us  [the longest x7 31.3 us: per_device(): lax.ppermute(going_down, ('rows', 'cols'), [(d, (d - 1) % ways) for d in...]
    ppermute x0 -> x15, waiting for transfers between devices: none -> 21.8 us  [the longest x8 21.5 us: per_device(): lax.ppermute(going_up, ('rows', 'cols'), [(d, (d + 1) % ways) for d in ra...]
    ppermute x2, waiting for transfers between devices: 7.79 us -> 0.39 us  [padded(): lax.ppermute(head, axis, [((i + 1) % count, i) for i in range(ends)])]
    ppermute x2, starting transfers between devices: 6.25 us -> 8.62 us  [padded(): lax.ppermute(tail, axis, [(i, (i + 1) % count) for i in range(ends)])]
    dot_general x1, matrix products: 3.13 us -> 1.6 us  [per_device(): jnp.einsum('qc,kc->qk', queries, key_rows, preferred_element_type=jnp.flo...]
    ppermute x2, waiting for transfers between devices: 0.66 us -> 2.08 us  [padded(): lax.ppermute(tail, axis, [(i, (i + 1) % count) for i in range(ends)])]
    broadcast_in_dim x1, other arithmetic: 1.18 us -> 0.26 us  [per_device(): rimmed[None]]
  transfers between devices with their start and end apart: 5 -> 19, of which waited for: 4 -> 13; matrix products, arithmetic and copies ran while one was open for 1% -> 1% of each run, Pallas kernels for 0% -> 0%
where the time goes in v1:
time: 86.2 us; the launch traced here: 85.8 us
  starting transfers between devices  44.3 us (51%)
  waiting for transfers between devices  24.3 us (28%)
  matrix products  10.4 us (12%)
  other arithmetic  4.6 us (5%)
  local copies, waits for them, and re-layouts  1.58 us (2%)
    ppermute x7, starting transfers between devices, per_device(): lax.ppermute(going_down, ('rows', 'cols'), [(d, (d - 1) % ways) for d in...  31.3 us
    ppermute x8, waiting for transfers between devices, per_device(): lax.ppermute(going_up, ('rows', 'cols'), [(d, (d + 1) % ways) for d in ra...  21.5 us
    ppermute x2, starting transfers between devices, padded(): lax.ppermute(tail, axis, [(i, (i + 1) % count) for i in range(ends)])  8.62 us
    conv_general_dilated x1, matrix products, per_device(): lax.conv_general_dilated(rimmed[None], conv_weight, (1, 1, 1), 'VALID', d...  5.2 us
    ppermute x2, starting transfers between devices, padded(): lax.ppermute(head, axis, [((i + 1) % count, i) for i in range(ends)])  2.58 us
    dot_general x1, matrix products, per_device(): jnp.dot(expos.astype(jnp.bfloat16), value_rows, preferred_element_type=jn...  2.56 us
    ppermute x2, waiting for transfers between devices, padded(): lax.ppermute(tail, axis, [(i, (i + 1) % count) for i in range(ends)])  2.08 us
    ppermute x8, starting transfers between devices, per_device(): lax.ppermute(going_up, ('rows', 'cols'), [(d, (d + 1) % ways) for d in ra...  1.75 us
  transfers between devices with their start and end apart: 19, of which 13 were waited for; matrix products, arithmetic and copies ran while one was open for 1% of the time, Pallas kernels for 0%

profile of v1, /device:TPU:0, one launch (start us, length us, event | category | flops | bytes accessed | tf_op | source)
XLA Modules:
  0.0 85.8 jit_solution(5190045588896250300)
XLA Ops:
  3.0 1.3 %collective-permute-start.1 = (bf16[3,1,32,384]{3,2,1,0:T(8,128)(2,1)S(1)}, bf16[3,1,32,384]{3,2,1,0:T(8,128)(2,1)S(1)}, u32[]{:S(2)}, u32[]{:S(2)}) collective-permute-start(bf16[3,1,32,384]{3,2,1,0:T(8,128)(2,1)S(1)} %get-tuple-element.10), channel_id=1, source_target_pairs={{4,0},{8,4},{12,8},{5,1},{9,5},{13,9},{6,2},{10,6},{14,10},{7,3},{... | collective-permute-start | bytes 221192 | tf_op jit(solution)/shard_map/ppermute | solution.py:19
  4.3 5.6 %collective-permute-start = (bf16[3,1,32,384]{3,2,1,0:T(8,128)(2,1)S(1)}, bf16[3,1,32,384]{3,2,1,0:T(8,128)(2,1)S(1)}, u32[]{:S(2)}, u32[]{:S(2)}) collective-permute-start(bf16[3,1,32,384]{3,2,1,0:T(8,128)(2,1)S(1)} %get-tuple-element.9), channel_id=1, source_target_pairs={{0,4},{4,8},{8,12},{1,5},{5,9},{9,13},{2,6},{6,10},{10,14},{3,7},{... | collective-permute-start | bytes 221192 | tf_op jit(solution)/shard_map/ppermute | solution.py:17
  10.2 1.6 %collective-permute-done = bf16[3,1,32,384]{3,2,1,0:T(8,128)(2,1)S(1)} collective-permute-done((bf16[3,1,32,384]{3,2,1,0:T(8,128)(2,1)S(1)}, bf16[3,1,32,384]{3,2,1,0:T(8,128)(2,1)S(1)}, u32[]{:S(2)}, u32[]{:S(2)}) %collective-permute-start) | collective-permute-done | bytes 73760 | tf_op jit(solution)/shard_map/ppermute | solution.py:17
  12.7 1.3 %collective-permute-start.3 = (bf16[3,6,1,384]{3,2,1,0:T(2,128)(2,1)S(1)}, bf16[3,6,1,384]{3,2,1,0:T(2,128)(2,1)S(1)}, u32[]{:S(2)}, u32[]{:S(2)}) collective-permute-start(bf16[3,6,1,384]{3,2,1,0:T(2,128)(2,1)S(1)} %get-tuple-element.8), channel_id=1, source_target_pairs={{1,0},{2,1},{3,2},{5,4},{6,5},{7,6},{9,8},{10,9},{11,10},{13,12},{... | collective-permute-start | bytes 41480 | tf_op jit(solution)/shard_map/ppermute | solution.py:19
  14.0 3.0 %collective-permute-start.2 = (bf16[3,6,1,384]{3,2,1,0:T(2,128)(2,1)S(1)}, bf16[3,6,1,384]{3,2,1,0:T(2,128)(2,1)S(1)}, u32[]{:S(2)}, u32[]{:S(2)}) collective-permute-start(bf16[3,6,1,384]{3,2,1,0:T(2,128)(2,1)S(1)} %get-tuple-element.7), channel_id=1, source_target_pairs={{0,1},{1,2},{2,3},{4,5},{5,6},{6,7},{8,9},{9,10},{10,11},{12,13},{... | collective-permute-start | bytes 41480 | tf_op jit(solution)/shard_map/ppermute | solution.py:17
  18.9 5.2 %convolution_select_fusion = f32[1,4,8,5,384]{4,2,3,1,0:T(8,128)S(1)} fusion(bf16[3,3,3,384,384]{4,3,2,1,0:T(8,128)(2,1)} %param.18, bf16[3,6,1,7,2,384]{5,3,4,1,0,2:T(8,128)(2,1)S(1)} %slice.18, bf16[3,6,1,8,5,384]{5,3,4,1,0,2:T(8,128)(2,1)S(1)} %copy.41, pred[8,5]{0,1:T(8,128)(4,1)S(1)} %copy-done.10), kind=kOutput, calls=%fused_computation.9 | convolution fusion | flops 1276403712 | bytes 8954920 | tf_op jit(solution)/shard_map/conv_general_dilated | solution.py:57
  24.9 1.7 %collective-permute-start.4 = (bf16[128,384]{1,0:T(8,128)(2,1)S(1)}, bf16[128,384]{1,0:T(8,128)(2,1)S(1)}, u32[]{:S(2)}, u32[]{:S(2)}) collective-permute-start(bf16[128,384]{1,0:T(8,128)(2,1)S(1)} %get-tuple-element.6), channel_id=1, source_target_pairs={{0,1},{1,2},{2,3},{3,4},{4,5},{5,6},{6,7},{7,8},{8,9},{9,10},{10,1... | collective-permute-start | bytes 294920 | tf_op jit(solution)/shard_map/ppermute | solution.py:89
  26.6 4.1 %collective-permute-start.5 = (bf16[128,384]{1,0:T(8,128)(2,1)S(1)}, bf16[128,384]{1,0:T(8,128)(2,1)S(1)}, u32[]{:S(2)}, u32[]{:S(2)}) collective-permute-start(bf16[128,384]{1,0:T(8,128)(2,1)S(1)} %get-tuple-element.6), channel_id=1, source_target_pairs={{0,15},{1,0},{2,1},{3,2},{4,3},{5,4},{6,5},{7,6},{8,7},{9,8},{10,9... | collective-permute-start | bytes 294920 | tf_op jit(solution)/shard_map/ppermute | solution.py:94
  31.0 2.1 %collective-permute-done.4 = bf16[128,384]{1,0:T(8,128)(2,1)S(1)} collective-permute-done((bf16[128,384]{1,0:T(8,128)(2,1)S(1)}, bf16[128,384]{1,0:T(8,128)(2,1)S(1)}, u32[]{:S(2)}, u32[]{:S(2)}) %collective-permute-start.4) | collective-permute-done | bytes 98336 | tf_op jit(solution)/shard_map/ppermute | solution.py:89
  33.1 4.4 %collective-permute-start.7 = (bf16[128,384]{1,0:T(8,128)(2,1)S(1)}, bf16[128,384]{1,0:T(8,128)(2,1)S(1)}, u32[]{:S(2)}, u32[]{:S(2)}) collective-permute-start(bf16[128,384]{1,0:T(8,128)(2,1)S(1)} %collective-permute-done.5), channel_id=1, source_target_pairs={{0,15},{1,0},{2,1},{3,2},{4,3},{5,4},{6,5},{7,6},{8,7},{9,8},{10,9... | collective-permute-start | bytes 294920 | tf_op jit(solution)/shard_map/ppermute | solution.py:94
  37.6 2.2 %collective-permute-done.6 = bf16[128,384]{1,0:T(8,128)(2,1)S(1)} collective-permute-done((bf16[128,384]{1,0:T(8,128)(2,1)S(1)}, bf16[128,384]{1,0:T(8,128)(2,1)S(1)}, u32[]{:S(2)}, u32[]{:S(2)}) %collective-permute-start.6) | collective-permute-done | bytes 98336 | tf_op jit(solution)/shard_map/ppermute | solution.py:89
  39.8 4.5 %collective-permute-start.9 = (bf16[128,384]{1,0:T(8,128)(2,1)S(1)}, bf16[128,384]{1,0:T(8,128)(2,1)S(1)}, u32[]{:S(2)}, u32[]{:S(2)}) collective-permute-start(bf16[128,384]{1,0:T(8,128)(2,1)S(1)} %collective-permute-done.7), channel_id=1, source_target_pairs={{0,15},{1,0},{2,1},{3,2},{4,3},{5,4},{6,5},{7,6},{8,7},{9,8},{10,9... | collective-permute-start | bytes 294920 | tf_op jit(solution)/shard_map/ppermute | solution.py:94
  44.4 2.2 %collective-permute-done.8 = bf16[128,384]{1,0:T(8,128)(2,1)S(1)} collective-permute-done((bf16[128,384]{1,0:T(8,128)(2,1)S(1)}, bf16[128,384]{1,0:T(8,128)(2,1)S(1)}, u32[]{:S(2)}, u32[]{:S(2)}) %collective-permute-start.8) | collective-permute-done | bytes 98336 | tf_op jit(solution)/shard_map/ppermute | solution.py:89
  46.7 4.4 %collective-permute-start.11 = (bf16[128,384]{1,0:T(8,128)(2,1)S(1)}, bf16[128,384]{1,0:T(8,128)(2,1)S(1)}, u32[]{:S(2)}, u32[]{:S(2)}) collective-permute-start(bf16[128,384]{1,0:T(8,128)(2,1)S(1)} %collective-permute-done.9), channel_id=1, source_target_pairs={{0,15},{1,0},{2,1},{3,2},{4,3},{5,4},{6,5},{7,6},{8,7},{9,8},{10,9... | collective-permute-start | bytes 294920 | tf_op jit(solution)/shard_map/ppermute | solution.py:94
  51.1 2.2 %collective-permute-done.10 = bf16[128,384]{1,0:T(8,128)(2,1)S(1)} collective-permute-done((bf16[128,384]{1,0:T(8,128)(2,1)S(1)}, bf16[128,384]{1,0:T(8,128)(2,1)S(1)}, u32[]{:S(2)}, u32[]{:S(2)}) %collective-permute-start.10) | collective-permute-done | bytes 98336 | tf_op jit(solution)/shard_map/ppermute | solution.py:89
  53.4 4.5 %collective-permute-start.13 = (bf16[128,384]{1,0:T(8,128)(2,1)S(1)}, bf16[128,384]{1,0:T(8,128)(2,1)S(1)}, u32[]{:S(2)}, u32[]{:S(2)}) collective-permute-start(bf16[128,384]{1,0:T(8,128)(2,1)S(1)} %collective-permute-done.11), channel_id=1, source_target_pairs={{0,15},{1,0},{2,1},{3,2},{4,3},{5,4},{6,5},{7,6},{8,7},{9,8},{10,9... | collective-permute-start | bytes 294920 | tf_op jit(solution)/shard_map/ppermute | solution.py:94
  58.0 2.1 %collective-permute-done.12 = bf16[128,384]{1,0:T(8,128)(2,1)S(1)} collective-permute-done((bf16[128,384]{1,0:T(8,128)(2,1)S(1)}, bf16[128,384]{1,0:T(8,128)(2,1)S(1)}, u32[]{:S(2)}, u32[]{:S(2)}) %collective-permute-start.12) | collective-permute-done | bytes 98336 | tf_op jit(solution)/shard_map/ppermute | solution.py:89
  60.2 4.6 %collective-permute-start.15 = (bf16[128,384]{1,0:T(8,128)(2,1)S(1)}, bf16[128,384]{1,0:T(8,128)(2,1)S(1)}, u32[]{:S(2)}, u32[]{:S(2)}) collective-permute-start(bf16[128,384]{1,0:T(8,128)(2,1)S(1)} %collective-permute-done.13), channel_id=1, source_target_pairs={{0,15},{1,0},{2,1},{3,2},{4,3},{5,4},{6,5},{7,6},{8,7},{9,8},{10,9... | collective-permute-start | bytes 294920 | tf_op jit(solution)/shard_map/ppermute | solution.py:94
  64.8 2.1 %collective-permute-done.14 = bf16[128,384]{1,0:T(8,128)(2,1)S(1)} collective-permute-done((bf16[128,384]{1,0:T(8,128)(2,1)S(1)}, bf16[128,384]{1,0:T(8,128)(2,1)S(1)}, u32[]{:S(2)}, u32[]{:S(2)}) %collective-permute-start.14) | collective-permute-done | bytes 98336 | tf_op jit(solution)/shard_map/ppermute | solution.py:89
  67.0 4.6 %collective-permute-start.17 = (bf16[128,384]{1,0:T(8,128)(2,1)S(1)}, bf16[128,384]{1,0:T(8,128)(2,1)S(1)}, u32[]{:S(2)}, u32[]{:S(2)}) collective-permute-start(bf16[128,384]{1,0:T(8,128)(2,1)S(1)} %collective-permute-done.15), channel_id=1, source_target_pairs={{0,15},{1,0},{2,1},{3,2},{4,3},{5,4},{6,5},{7,6},{8,7},{9,8},{10,9... | collective-permute-start | bytes 294920 | tf_op jit(solution)/shard_map/ppermute | solution.py:94
  71.7 2.0 %collective-permute-done.16 = bf16[128,384]{1,0:T(8,128)(2,1)S(1)} collective-permute-done((bf16[128,384]{1,0:T(8,128)(2,1)S(1)}, bf16[128,384]{1,0:T(8,128)(2,1)S(1)}, u32[]{:S(2)}, u32[]{:S(2)}) %collective-permute-start.16) | collective-permute-done | bytes 98336 | tf_op jit(solution)/shard_map/ppermute | solution.py:89
  73.8 6.5 %collective-permute-done.18 = bf16[128,384]{1,0:T(8,128)(2,1)S(1)} collective-permute-done((bf16[128,384]{1,0:T(8,128)(2,1)S(1)}, bf16[128,384]{1,0:T(8,128)(2,1)S(1)}, u32[]{:S(2)}, u32[]{:S(2)}) %collective-permute-start.18) | collective-permute-done | bytes 98336 | tf_op jit(solution)/shard_map/ppermute | solution.py:89
  80.4 1.6 %fusion.36 = (f32[128]{0:T(128)S(1)}, f32[128,2048]{1,0:T(8,128)S(1)}) fusion(bf16[128,384]{1,0:T(8,128)(2,1)S(1)} %fusion.3, bf16[2048,384]{1,0:T(8,128)(2,1)S(1)} %constant_dynamic-update-slice_fusion, bf16[384,384]{1,0:T(8,128)(2,1)S(1)} %copy-done), kind=kOutput, calls=%fused_computation.73 | convolution fusion | flops 806616960 | bytes 3015168 | tf_op jit(solution)/shard_map/qc,kc->qk/dot_general | solution.py:106
  82.4 2.6 %fusion.6 = bf16[128,384]{1,0:T(8,128)(2,1)S(1)} fusion(bf16[2048,384]{1,0:T(8,128)(2,1)S(1)} %constant_dynamic-update-slice_fusion, bf16[384,384]{1,0:T(8,128)(2,1)} %param.24, f32[384]{0:T(512)S(1)} %copy-done.9, f32[128,2048]{1,0:T(8,128)S(1)} %get-tuple-element.13, f32[128]{0:T(128)S(1)} %broadcast_maximum_fusion, f32[128]{0:T(128)S(1)} %fusion.7), kind=kOutput, calls=%fused_computation.13 | convolution fusion | flops 807501824 | bytes 3017216 | tf_op jit(solution)/shard_map/dot_general | solution.py:111
  (76 shorter events, 8.5 us)
Async XLA Ops:
  0.0 80.4 %copy-start = (bf16[384,384]{1,0:T(8,128)(2,1)S(1)}, bf16[384,384]{1,0:T(8,128)(2,1)}, u32[]{:S(2)}) copy-start(bf16[384,384]{1,0:T(8,128)(2,1)} %param.23) | copy-start | bytes 884740
  0.0 17.9 %copy-start.1 = (bf16[1,2,4,32,384]{4,3,2,1,0:T(8,128)(2,1)S(1)}, bf16[1,2,4,32,384]{4,3,2,1,0:T(8,128)(2,1)}, u32[]{:S(2)}) copy-start(bf16[1,2,4,32,384]{4,3,2,1,0:T(8,128)(2,1)} %param.15) | copy-start | bytes 589828
  3.0 7.3 %collective-permute-start.1 = (bf16[3,1,32,384]{3,2,1,0:T(8,128)(2,1)S(1)}, bf16[3,1,32,384]{3,2,1,0:T(8,128)(2,1)S(1)}, u32[]{:S(2)}, u32[]{:S(2)}) collective-permute-start(bf16[3,1,32,384]{3,2,1,0:T(8,128)(2,1)S(1)} %get-tuple-element.10), channel_id=1, source_target_pairs={{4,0},{8,4},{12,8},{5,1},{9,5},{13,9},{6,2},{10,6},{14,10},{7,3},{... | collective-permute-start | bytes 221192 | tf_op jit(solution)/shard_map/ppermute | solution.py:19
  4.3 7.6 %collective-permute-start = (bf16[3,1,32,384]{3,2,1,0:T(8,128)(2,1)S(1)}, bf16[3,1,32,384]{3,2,1,0:T(8,128)(2,1)S(1)}, u32[]{:S(2)}, u32[]{:S(2)}) collective-permute-start(bf16[3,1,32,384]{3,2,1,0:T(8,128)(2,1)S(1)} %get-tuple-element.9), channel_id=1, source_target_pairs={{0,4},{4,8},{8,12},{1,5},{5,9},{9,13},{2,6},{6,10},{10,14},{3,7},{... | collective-permute-start | bytes 221192 | tf_op jit(solution)/shard_map/ppermute | solution.py:17
  12.7 4.7 %collective-permute-start.3 = (bf16[3,6,1,384]{3,2,1,0:T(2,128)(2,1)S(1)}, bf16[3,6,1,384]{3,2,1,0:T(2,128)(2,1)S(1)}, u32[]{:S(2)}, u32[]{:S(2)}) collective-permute-start(bf16[3,6,1,384]{3,2,1,0:T(2,128)(2,1)S(1)} %get-tuple-element.8), channel_id=1, source_target_pairs={{1,0},{2,1},{3,2},{5,4},{6,5},{7,6},{9,8},{10,9},{11,10},{13,12},{... | collective-permute-start | bytes 41480 | tf_op jit(solution)/shard_map/ppermute | solution.py:19
  14.0 3.9 %collective-permute-start.2 = (bf16[3,6,1,384]{3,2,1,0:T(2,128)(2,1)S(1)}, bf16[3,6,1,384]{3,2,1,0:T(2,128)(2,1)S(1)}, u32[]{:S(2)}, u32[]{:S(2)}) collective-permute-start(bf16[3,6,1,384]{3,2,1,0:T(2,128)(2,1)S(1)} %get-tuple-element.7), channel_id=1, source_target_pairs={{0,1},{1,2},{2,3},{4,5},{5,6},{6,7},{8,9},{9,10},{10,11},{12,13},{... | collective-permute-start | bytes 41480 | tf_op jit(solution)/shard_map/ppermute | solution.py:17
  18.9 5.4 %copy-start.5 = (f32[384]{0:T(512)S(1)}, f32[384]{0:T(512)}, u32[]{:S(2)}) copy-start(f32[384]{0:T(512)} %param.19) | copy-start | bytes 4612
  24.2 6.5 %copy-start.4 = (bf16[384,384]{1,0:T(8,128)(2,1)S(1)}, bf16[384,384]{1,0:T(8,128)(2,1)}, u32[]{:S(2)}) copy-start(bf16[384,384]{1,0:T(8,128)(2,1)} %param.21) | copy-start | bytes 884740
  24.2 6.5 %copy-start.7 = (f32[384]{0:T(512)S(1)}, f32[384]{0:T(512)}, u32[]{:S(2)}) copy-start(f32[384]{0:T(512)} %param.22) | copy-start | bytes 4612
  24.9 8.2 %collective-permute-start.4 = (bf16[128,384]{1,0:T(8,128)(2,1)S(1)}, bf16[128,384]{1,0:T(8,128)(2,1)S(1)}, u32[]{:S(2)}, u32[]{:S(2)}) collective-permute-start(bf16[128,384]{1,0:T(8,128)(2,1)S(1)} %get-tuple-element.6), channel_id=1, source_target_pairs={{0,1},{1,2},{2,3},{3,4},{4,5},{5,6},{6,7},{7,8},{8,9},{9,10},{10,1... | collective-permute-start | bytes 294920 | tf_op jit(solution)/shard_map/ppermute | solution.py:89
  26.6 6.4 %collective-permute-start.5 = (bf16[128,384]{1,0:T(8,128)(2,1)S(1)}, bf16[128,384]{1,0:T(8,128)(2,1)S(1)}, u32[]{:S(2)}, u32[]{:S(2)}) collective-permute-start(bf16[128,384]{1,0:T(8,128)(2,1)S(1)} %get-tuple-element.6), channel_id=1, source_target_pairs={{0,15},{1,0},{2,1},{3,2},{4,3},{5,4},{6,5},{7,6},{8,7},{9,8},{10,9... | collective-permute-start | bytes 294920 | tf_op jit(solution)/shard_map/ppermute | solution.py:94
  33.1 6.7 %collective-permute-start.6 = (bf16[128,384]{1,0:T(8,128)(2,1)S(1)}, bf16[128,384]{1,0:T(8,128)(2,1)S(1)}, u32[]{:S(2)}, u32[]{:S(2)}) collective-permute-start(bf16[128,384]{1,0:T(8,128)(2,1)S(1)} %collective-permute-done.4), channel_id=1, source_target_pairs={{0,1},{1,2},{2,3},{3,4},{4,5},{5,6},{6,7},{7,8},{8,9},{9,10},{10,1... | collective-permute-start | bytes 294920 | tf_op jit(solution)/shard_map/ppermute | solution.py:89
  33.1 6.7 %collective-permute-start.7 = (bf16[128,384]{1,0:T(8,128)(2,1)S(1)}, bf16[128,384]{1,0:T(8,128)(2,1)S(1)}, u32[]{:S(2)}, u32[]{:S(2)}) collective-permute-start(bf16[128,384]{1,0:T(8,128)(2,1)S(1)} %collective-permute-done.5), channel_id=1, source_target_pairs={{0,15},{1,0},{2,1},{3,2},{4,3},{5,4},{6,5},{7,6},{8,7},{9,8},{10,9... | collective-permute-start | bytes 294920 | tf_op jit(solution)/shard_map/ppermute | solution.py:94
  39.8 6.8 %collective-permute-start.8 = (bf16[128,384]{1,0:T(8,128)(2,1)S(1)}, bf16[128,384]{1,0:T(8,128)(2,1)S(1)}, u32[]{:S(2)}, u32[]{:S(2)}) collective-permute-start(bf16[128,384]{1,0:T(8,128)(2,1)S(1)} %collective-permute-done.6), channel_id=1, source_target_pairs={{0,1},{1,2},{2,3},{3,4},{4,5},{5,6},{6,7},{7,8},{8,9},{9,10},{10,1... | collective-permute-start | bytes 294920 | tf_op jit(solution)/shard_map/ppermute | solution.py:89
  39.8 6.8 %collective-permute-start.9 = (bf16[128,384]{1,0:T(8,128)(2,1)S(1)}, bf16[128,384]{1,0:T(8,128)(2,1)S(1)}, u32[]{:S(2)}, u32[]{:S(2)}) collective-permute-start(bf16[128,384]{1,0:T(8,128)(2,1)S(1)} %collective-permute-done.7), channel_id=1, source_target_pairs={{0,15},{1,0},{2,1},{3,2},{4,3},{5,4},{6,5},{7,6},{8,7},{9,8},{10,9... | collective-permute-start | bytes 294920 | tf_op jit(solution)/shard_map/ppermute | solution.py:94
  46.6 6.7 %collective-permute-start.10 = (bf16[128,384]{1,0:T(8,128)(2,1)S(1)}, bf16[128,384]{1,0:T(8,128)(2,1)S(1)}, u32[]{:S(2)}, u32[]{:S(2)}) collective-permute-start(bf16[128,384]{1,0:T(8,128)(2,1)S(1)} %collective-permute-done.8), channel_id=1, source_target_pairs={{0,1},{1,2},{2,3},{3,4},{4,5},{5,6},{6,7},{7,8},{8,9},{9,10},{10,1... | collective-permute-start | bytes 294920 | tf_op jit(solution)/shard_map/ppermute | solution.py:89
  46.7 6.7 %collective-permute-start.11 = (bf16[128,384]{1,0:T(8,128)(2,1)S(1)}, bf16[128,384]{1,0:T(8,128)(2,1)S(1)}, u32[]{:S(2)}, u32[]{:S(2)}) collective-permute-start(bf16[128,384]{1,0:T(8,128)(2,1)S(1)} %collective-permute-done.9), channel_id=1, source_target_pairs={{0,15},{1,0},{2,1},{3,2},{4,3},{5,4},{6,5},{7,6},{8,7},{9,8},{10,9... | collective-permute-start | bytes 294920 | tf_op jit(solution)/shard_map/ppermute | solution.py:94
  53.4 6.7 %collective-permute-start.12 = (bf16[128,384]{1,0:T(8,128)(2,1)S(1)}, bf16[128,384]{1,0:T(8,128)(2,1)S(1)}, u32[]{:S(2)}, u32[]{:S(2)}) collective-permute-start(bf16[128,384]{1,0:T(8,128)(2,1)S(1)} %collective-permute-done.10), channel_id=1, source_target_pairs={{0,1},{1,2},{2,3},{3,4},{4,5},{5,6},{6,7},{7,8},{8,9},{9,10},{10,1... | collective-permute-start | bytes 294920 | tf_op jit(solution)/shard_map/ppermute | solution.py:89
  53.4 6.8 %collective-permute-start.13 = (bf16[128,384]{1,0:T(8,128)(2,1)S(1)}, bf16[128,384]{1,0:T(8,128)(2,1)S(1)}, u32[]{:S(2)}, u32[]{:S(2)}) collective-permute-start(bf16[128,384]{1,0:T(8,128)(2,1)S(1)} %collective-permute-done.11), channel_id=1, source_target_pairs={{0,15},{1,0},{2,1},{3,2},{4,3},{5,4},{6,5},{7,6},{8,7},{9,8},{10,9... | collective-permute-start | bytes 294920 | tf_op jit(solution)/shard_map/ppermute | solution.py:94
  60.1 6.8 %collective-permute-start.14 = (bf16[128,384]{1,0:T(8,128)(2,1)S(1)}, bf16[128,384]{1,0:T(8,128)(2,1)S(1)}, u32[]{:S(2)}, u32[]{:S(2)}) collective-permute-start(bf16[128,384]{1,0:T(8,128)(2,1)S(1)} %collective-permute-done.12), channel_id=1, source_target_pairs={{0,1},{1,2},{2,3},{3,4},{4,5},{5,6},{6,7},{7,8},{8,9},{9,10},{10,1... | collective-permute-start | bytes 294920 | tf_op jit(solution)/shard_map/ppermute | solution.py:89
  60.2 6.8 %collective-permute-start.15 = (bf16[128,384]{1,0:T(8,128)(2,1)S(1)}, bf16[128,384]{1,0:T(8,128)(2,1)S(1)}, u32[]{:S(2)}, u32[]{:S(2)}) collective-permute-start(bf16[128,384]{1,0:T(8,128)(2,1)S(1)} %collective-permute-done.13), channel_id=1, source_target_pairs={{0,15},{1,0},{2,1},{3,2},{4,3},{5,4},{6,5},{7,6},{8,7},{9,8},{10,9... | collective-permute-start | bytes 294920 | tf_op jit(solution)/shard_map/ppermute | solution.py:94
  66.9 6.7 %collective-permute-start.16 = (bf16[128,384]{1,0:T(8,128)(2,1)S(1)}, bf16[128,384]{1,0:T(8,128)(2,1)S(1)}, u32[]{:S(2)}, u32[]{:S(2)}) collective-permute-start(bf16[128,384]{1,0:T(8,128)(2,1)S(1)} %collective-permute-done.14), channel_id=1, source_target_pairs={{0,1},{1,2},{2,3},{3,4},{4,5},{5,6},{6,7},{7,8},{8,9},{9,10},{10,1... | collective-permute-start | bytes 294920 | tf_op jit(solution)/shard_map/ppermute | solution.py:89
  67.0 6.8 %collective-permute-start.17 = (bf16[128,384]{1,0:T(8,128)(2,1)S(1)}, bf16[128,384]{1,0:T(8,128)(2,1)S(1)}, u32[]{:S(2)}, u32[]{:S(2)}) collective-permute-start(bf16[128,384]{1,0:T(8,128)(2,1)S(1)} %collective-permute-done.15), channel_id=1, source_target_pairs={{0,15},{1,0},{2,1},{3,2},{4,3},{5,4},{6,5},{7,6},{8,7},{9,8},{10,9... | collective-permute-start | bytes 294920 | tf_op jit(solution)/shard_map/ppermute | solution.py:94
  73.6 6.7 %collective-permute-start.18 = (bf16[128,384]{1,0:T(8,128)(2,1)S(1)}, bf16[128,384]{1,0:T(8,128)(2,1)S(1)}, u32[]{:S(2)}, u32[]{:S(2)}) collective-permute-start(bf16[128,384]{1,0:T(8,128)(2,1)S(1)} %collective-permute-done.16), channel_id=1, source_target_pairs={{0,1},{1,2},{2,3},{3,4},{4,5},{5,6},{6,7},{7,8},{8,9},{9,10},{10,1... | collective-permute-start | bytes 294920 | tf_op jit(solution)/shard_map/ppermute | solution.py:89
  (6 other events, 13.8 us)
